TPU v7x, 128 devices: a whole 4x4x4 slice. The times are simulated.
128 devices in a mesh: slab: 8 (over y, x_hi), brick: 16 (over x_lo, z, core).
Axes of the slice: x: 4 (x_hi: 2, x_lo: 2; x = x_hi * 2 + x_lo), y: 4, z: 4, core: 2. Of those that a mesh axis runs over, the one named last changes fastest.
Arguments:
- k_coeffs: float32 [16, 32, 16, 128], P('slab', 'brick'), may hold values from -0.3 to 0.4
- v_basis: float32 [32768, 128], P(('slab', 'brick')), may hold values from -4 to 4
Outputs:
- basis_x: float32 [16, 32, 16, 128], P('slab', 'brick')
- coupling: float32 [128, 128], replicated
- basis_v: float32 [32768, 128], P(('slab', 'brick'))
All inputs are finite; a program needn't handle non-finite values.
Results may differ from a plain program's by a relative error of at most 0.0001.
Values sent between devices are 32-bit elements; how exact they have to be, the bound alone decides.
No kernel may reach another device: no remote copies, remote signals or barrier semaphores. Data moves between devices by JAX's collectives and lax.ppermute only.
A program may use at most 64 MiB of HBM per device.

v0:
```python
import math
import jax
import jax.numpy as jnp
from jax import lax
from jax.sharding import PartitionSpec as P

NVX = 32
CFL = 0.9
VMAX = 6.0
COLLIDE = 0.3
RHO_MIN = 0.25
TEMP_MIN = 0.25
PRECISE = lax.Precision.HIGHEST


def with_halo(array, sides, width):
    edges = {}
    for axis, dim in sides:
        peers, length = (lax.axis_size(axis), array.shape[dim])
        up = [(i, (i + 1) % peers) for i in range(peers)]
        last = lax.slice_in_dim(array, length - width, length, axis=dim)
        leading = lax.slice_in_dim(array, 0, width, axis=dim)
        edges[dim] = (
            lax.ppermute(last, axis, up),
            lax.ppermute(leading, axis, [(b, a) for a, b in up]),
        )
    done = []
    for _, dim in sides:
        low, high = edges[dim]
        around = [(width, width) if d in done else (0, 0) for d in range(array.ndim)]
        array = jnp.concatenate([jnp.pad(low, around), array, jnp.pad(high, around)], axis=dim)
        done.append(dim)
    return array


def over_pieces(array, axis):
    parts = lax.all_gather(array, axis)
    return parts.sum(axis=0)


def velocities(indices):
    spacing = 2.0 * VMAX / NVX
    first_index = indices // (NVX * NVX)
    second = indices // NVX % NVX
    third_index = indices % NVX
    coords = jnp.stack([first_index, second, third_index]).astype(jnp.float32)
    return -VMAX + (coords + 0.5) * spacing


def maxwell(cell_params, velocity):
    distance = (velocity[0][None, :] - cell_params[1][:, None]) ** 2
    distance = distance + (velocity[1][None, :] - cell_params[2][:, None]) ** 2
    distance = distance + (velocity[2][None, :] - cell_params[3][:, None]) ** 2
    amplitude = cell_params[0] * (2.0 * math.pi * cell_params[4]) ** (-1.5)
    return amplitude[:, None] * jnp.exp(distance * (-0.5 / cell_params[4])[:, None])


def cell_state(vectors, coeffs):
    moments = lax.dot_general(vectors, coeffs, (((1,), (1,)), ((), ())), precision=PRECISE)
    density = jnp.maximum(moments[0], RHO_MIN)
    drift_speed = moments[1:4] / density[None, :]
    temper = jnp.maximum(
        (moments[4] / density - jnp.sum(drift_speed * drift_speed, axis=0)) / 3.0, TEMP_MIN
    )
    return jnp.concatenate([density[None], drift_speed, temper[None]], axis=0)


def transport_flux(backward, forward, transport):
    flux = jnp.zeros_like(backward[0])
    for axis_id in range(3):
        flux = flux + jnp.dot(backward[axis_id], transport[axis_id], precision=PRECISE)
        flux = flux + jnp.dot(forward[axis_id], transport[3 + axis_id], precision=PRECISE)
    return flux


def products(left_side, backward, forward, maxwell_proj):
    pieces = [
        lax.dot_general(left_side, item, (((0,), (0,)), ((), ())), precision=PRECISE)
        for item in backward + forward + [maxwell_proj]
    ]
    return jnp.stack(pieces)


def coupling_step(coupling_hat, minus_side, plus_side, projected, transport, time_step):
    drift_sum = jnp.zeros_like(coupling_hat)
    for axis_id in range(3):
        drift_sum = drift_sum + jnp.dot(
            jnp.dot(minus_side[axis_id], coupling_hat, precision=PRECISE),
            transport[axis_id],
            precision=PRECISE,
        )
        drift_sum = drift_sum + jnp.dot(
            jnp.dot(plus_side[axis_id], coupling_hat, precision=PRECISE),
            transport[3 + axis_id],
            precision=PRECISE,
        )
    return coupling_hat + time_step * drift_sum - COLLIDE * (projected - coupling_hat)


def velocity_step(velocity_part, minus_side, plus_side, back_proj, positive, negative, time_step):
    drift_sum = jnp.zeros_like(velocity_part)
    for axis_id in range(3):
        drift_sum = drift_sum + positive[axis_id][:, None] * jnp.dot(
            velocity_part, minus_side[axis_id].T, precision=PRECISE
        )
        drift_sum = drift_sum + negative[axis_id][:, None] * jnp.dot(
            velocity_part, plus_side[axis_id].T, precision=PRECISE
        )
    return velocity_part - time_step * drift_sum + COLLIDE * (back_proj - velocity_part)


def slopes(padded, lengths):
    rank_size = padded.shape[3]
    centre = padded[1:-1, 1:-1]
    backward = [
        (centre - padded[:-2, 1:-1]) * lengths[0],
        (centre - padded[1:-1, :-2]) * lengths[1],
        (centre - jnp.roll(centre, 1, axis=2)) * lengths[2],
    ]
    forward = [
        (padded[2:, 1:-1] - centre) * lengths[0],
        (padded[1:-1, 2:] - centre) * lengths[1],
        (jnp.roll(centre, -1, axis=2) - centre) * lengths[2],
    ]
    return (
        [item.reshape(-1, rank_size) for item in backward],
        [item.reshape(-1, rank_size) for item in forward],
    )


def local(k_coeffs, v_basis):
    cells_x, cells_y, cells_z, rank_size = k_coeffs.shape
    cell_count = cells_x * cells_y * cells_z
    slab_count = lax.axis_size("slab")
    brick_count = lax.axis_size("brick")
    devices = slab_count * brick_count
    lengths = (cells_x * slab_count, cells_y * brick_count, cells_z)
    time_step = CFL / (VMAX * (lengths[0] + lengths[1] + lengths[2]))
    weight_x = 1.0 / (lengths[0] * lengths[1] * lengths[2])
    weight_v = (2.0 * VMAX / NVX) ** 3
    row_count = v_basis.shape[0]
    device = lax.axis_index("slab") * brick_count + lax.axis_index("brick")
    row_ids = device * row_count + jnp.arange(row_count, dtype=jnp.int32)
    velocity = velocities(row_ids)
    positive = jnp.maximum(velocity, 0.0)
    negative = jnp.minimum(velocity, 0.0)
    weights = jnp.stack(
        [
            jnp.ones_like(velocity[0]),
            velocity[0],
            velocity[1],
            velocity[2],
            jnp.sum(velocity * velocity, axis=0),
        ]
    )
    vectors = jnp.dot(weights, v_basis, precision=PRECISE) * weight_v
    transport = jnp.stack(
        [
            lax.dot_general(
                v_basis * (side[axis_id] * weight_v)[:, None],
                v_basis,
                (((0,), (0,)), ((), ())),
                precision=PRECISE,
            )
            for side in (positive, negative)
            for axis_id in range(3)
        ]
    )
    transport, vectors = lax.psum((transport, vectors), ("slab", "brick"))
    coeff_flat = k_coeffs.reshape(cell_count, rank_size)
    cell_params = cell_state(vectors, coeff_flat)
    params_all = lax.all_gather(cell_params, ("slab", "brick"), axis=1, tiled=True)
    row_total = cell_count * devices
    block_rows = math.gcd(row_total, 512)

    def one_block(turn_index):
        part_params = lax.dynamic_slice_in_dim(
            params_all, 0 + turn_index * block_rows, block_rows, 1
        )
        return jnp.dot(maxwell(part_params, velocity), v_basis, precision=PRECISE) * weight_v

    blocks = lax.map(one_block, jnp.arange(row_total // block_rows, dtype=jnp.int32))
    whole_term = lax.psum(blocks.reshape(row_total, rank_size), ("slab", "brick"))
    maxwell_proj = lax.dynamic_slice_in_dim(whole_term, device * cell_count, cell_count, 0)
    padded = with_halo(k_coeffs, (("slab", 0), ("brick", 1)), 1)
    backward, forward = slopes(padded, lengths)
    advanced = (
        coeff_flat
        - time_step * transport_flux(backward, forward, transport)
        + COLLIDE * (maxwell_proj - coeff_flat)
    )
    identity = jnp.eye(rank_size, dtype=jnp.float32)
    padded_new = with_halo(
        advanced.reshape(cells_x, cells_y, cells_z, rank_size), (("slab", 0), ("brick", 1)), 1
    )
    backward, forward = slopes(padded_new, lengths)
    local_sums = jnp.concatenate(
        [
            lax.dot_general(advanced, advanced, (((0,), (0,)), ((), ())), precision=PRECISE)[None],
            products(advanced, backward, forward, maxwell_proj),
        ],
        axis=0,
    )
    reduced_all = lax.psum(local_sums * weight_x, ("slab", "brick"))
    factor = jnp.linalg.cholesky(reduced_all[0])
    inverse = jax.scipy.linalg.solve_triangular(factor, identity, lower=True)
    basis_new = jnp.dot(advanced, inverse.T, precision=PRECISE)
    mapped = jnp.einsum("ab,kbc,dc->kad", inverse, reduced_all[1:7], inverse, precision=PRECISE)
    minus_side = mapped[0:3]
    plus_side = mapped[3:6]
    projected = jnp.dot(inverse, reduced_all[7], precision=PRECISE)
    coupling_mid = coupling_step(factor.T, minus_side, plus_side, projected, transport, time_step)
    rows_piece = lax.all_gather(basis_new, ("slab", "brick"), axis=0, tiled=True)
    piece_rows = rows_piece.shape[0]
    fold_block_rows = math.gcd(piece_rows, 512)

    def add_block(turn_index, accumulated):
        offset = turn_index * fold_block_rows
        part_params = lax.dynamic_slice_in_dim(params_all, offset, fold_block_rows, 1)
        basis_block = lax.dynamic_slice_in_dim(rows_piece, offset, fold_block_rows, 0)
        values = maxwell(part_params, velocity)
        return (
            accumulated
            + lax.dot_general(values, basis_block, (((0,), (0,)), ((), ())), precision=PRECISE)
            * weight_x
        )

    back_proj = lax.fori_loop(
        0, piece_rows // fold_block_rows, add_block, jnp.zeros((row_count, rank_size), jnp.float32)
    )
    velocity_part = jnp.dot(v_basis, coupling_mid.T, precision=PRECISE)
    velocity_new = velocity_step(
        velocity_part, minus_side, plus_side, back_proj, positive, negative, time_step
    )
    gram_v = (
        lax.dot_general(velocity_new, velocity_new, (((0,), (0,)), ((), ())), precision=PRECISE)
        * weight_v
    )
    gram_v = over_pieces(gram_v, ("slab", "brick"))
    coupling = jnp.linalg.cholesky(gram_v)
    inverse_v = jax.scipy.linalg.solve_triangular(coupling, identity, lower=True)
    vbasis_new = jnp.dot(velocity_new, inverse_v.T, precision=PRECISE)
    return (basis_new.reshape(cells_x, cells_y, cells_z, rank_size), coupling, vbasis_new)


def solution(mesh):
    placed = (P("slab", "brick", None, None), P(("slab", "brick"), None))
    return jax.shard_map(
        local,
        mesh=mesh,
        in_specs=placed,
        out_specs=(P("slab", "brick", None, None), P(), P(("slab", "brick"), None)),
        check_vma=False,
    )
```

profile of v0, /device:TPU:1, one launch (start us, length us, event | category | flops | bytes accessed | tf_op | source)
XLA Modules:
  0.0 735.6 jit_solution(13024606328633485945)
XLA Ops:
  8.4 68.7 %psum.29 = f32[5,128]{1,0:T(8,128)S(1)} all-reduce(f32[5,128]{1,0:T(8,128)S(1)} %convolution_multiply_fusion.9), channel_id=1, replica_groups=mesh['slab'=8,'brick'=16] {'slab','brick'}, use_global_device_ids=true, to_apply=%region_2.3 | all-reduce | flops 640 | bytes 5120 | tf_op jit(solution)/shard_map/psum | solution.py:169
  78.1 34.4 %all-gather.1 = f32[128,64,5]{1,2,0:T(8,128)S(1)} all-gather(f32[1,64,5]{1,2,0:T(8,128)S(1)} %maximum_bitcast_fusion), channel_id=1, replica_groups=mesh['slab'=8,'brick'=16] {'slab','brick'}, dimensions={0}, use_global_device_ids=true | all-gather | bytes 165120 | tf_op jit(solution)/shard_map/all_gather | solution.py:172
  112.7 60.6 %while.24 = (s32[]{:T(128)}, f32[16,512,128]{2,1,0:T(8,128)}, s32[16]{0:T(128)S(1)}, f32[5,8192]{1,0:T(8,128)S(1)}, f32[3,256]{1,0:T(4,128)S(1)}, /*index=5*/f32...) while((s32[]{:T(128)}, f32[16,512,128]{2,1,0:T(8,128)}, ...), condition=%wide.region_5.6_spmd, body=%wide.region_4.5_spmd.sunk | while | flops 202704400 | bytes 433923 | solution.py:182
  114.1 2.5 fusion.232
  117.9 2.4 fusion.232
  121.7 2.4 fusion.232
  136.8 2.4 fusion.232
  144.3 2.4 fusion.232
  151.9 2.4 fusion.232
  155.7 2.4 fusion.232
  167.0 2.5 fusion.232
  170.8 2.4 fusion.232
  184.1 3.9 collective-permute-start.1
  191.7 143.5 %all-reduce.10.cloned.1.call-done = (f32[6,128,128]{2,1,0:T(8,128)}, f32[8192,128]{1,0:T(8,128)}) async-done(((f32[6,128,128]{2,1,0:T(8,128)}, f32[8192,128]{1,0:T(8,128)}), (f32[6,128,128]{2,1,0:T(8,128)}, f32[8192,128]{1,0:T(8,128)})) %all-reduce.10.cloned.1.call-update) | async-done | bytes 4587536 | tf_op jit(solution)/shard_map/psum | solution.py:169
  344.1 4.2 collective-permute-start.6
  355.3 144.6 %all-reduce.8.cloned.1.call-done = f32[8,128,128]{1,2,0:T(8,128)} async-done(((f32[8,128,128]{1,2,0:T(8,128)}), f32[8,128,128]{1,2,0:T(8,128)}) %all-reduce.8.cloned.1.call-update) | async-done | bytes 524304 | tf_op jit(solution)/shard_map/psum | solution.py:204
  501.6 11.7 %cholesky.44 = f32[128,128]{1,0:T(8,128)S(1)} custom-call(f32[128,128]{1,0:T(8,128)S(1)} %fusion.83), custom_call_target="Cholesky" | custom-call | tf_op jit(solution)/shard_map/jit(cholesky)/cholesky | solution.py:205
  514.7 9.8 %custom-call.7 = f32[1,128,128]{1,2,0:T(8,128)S(1)} custom-call(f32[1,128,128]{2,1,0:T(8,128)S(1)} %select_bitcast_fusion.1), custom_call_target="InvertDiagBlocksLowerTriangular" | custom-call | tf_op jit(solution)/shard_map/jit(_solve_triangular)/triangular_solve | solution.py:206
  539.1 52.7 %all-gather.5.cloned.1.call-done = f32[8192,128]{1,0:T(8,128)} async-done(((f32[64,128]{1,0:T(8,128)}), f32[8192,128]{1,0:T(8,128)}) %all-gather.5.cloned.1.call-update) | async-done | bytes 4194320 | tf_op jit(solution)/shard_map/all_gather | solution.py:213
  591.8 39.5 %while.25 = (s32[]{:T(128)}, f32[256,128]{1,0:T(8,128)S(1)}, f32[5,8192]{1,0:T(8,128)S(1)}, f32[3,256]{1,0:T(4,128)S(1)}, f32[8192,128]{1,0:T(8,128)}, /*index=5...) while((s32[]{:T(128)}, f32[256,128]{1,0:T(8,128)S(1)}, ...), condition=%wide.region_11.14_spmd.clone, body=%wide.region_10.13_spmd.clone.sunk | while | flops 202737168 | bytes 564477 | solution.py:228
  632.6 67.7 %all-gather.7.cloned.1.call-done = f32[16384,128]{1,0:T(8,128)} async-done(((f32[128,128]{1,0:T(8,128)}), f32[16384,128]{1,0:T(8,128)}) %all-gather.7.cloned.1.call-update) | async-done | bytes 8388624 | tf_op jit(solution)/shard_map/all_gather | solution.py:37
  700.3 3.8 reduce_sum.32
  704.3 11.7 %cholesky.55 = f32[128,128]{1,0:T(8,128)S(1)} custom-call(f32[128,128]{1,0:T(8,128)S(1)} %fusion.85), custom_call_target="Cholesky" | custom-call | tf_op jit(solution)/shard_map/jit(cholesky)/cholesky | solution.py:240
  717.9 9.8 %custom-call.8 = f32[1,128,128]{1,2,0:T(8,128)S(1)} custom-call(f32[1,128,128]{2,1,0:T(8,128)S(1)} %get-tuple-element.175), custom_call_target="InvertDiagBlocksLowerTriangular" | custom-call | tf_op jit(solution)/shard_map/jit(_solve_triangular)/triangular_solve | solution.py:241
  (232 shorter events, 121.4 us)
Async XLA Ops:
  7.2 328.0 %all-reduce.10.cloned.1.call-start = ((), (), s32[]{:S(2)}) async-start(), calls=%async_computation.3 | async-start | bytes 9175040 | tf_op jit(solution)/shard_map/psum | solution.py:169
  173.3 9.6 %copy-start.1 = (f32[2,2,16,128]{3,2,1,0:T(8,128)S(1)}, f32[2,2,16,128]{3,2,1,0:T(8,128)}, u32[]{:S(2)}) copy-start(f32[2,2,16,128]{3,2,1,0:T(8,128)} %param.9) | copy-start | bytes 98308
  182.0 0.8 copy-start.3
  182.8 317.0 %all-reduce.8.cloned.1.call-start = ((), (), s32[]{:S(2)}) async-start(), calls=%async_computation | async-start | bytes 1048576 | tf_op jit(solution)/shard_map/psum | solution.py:204
  182.9 6.3 collective-permute-start
  184.1 5.0 collective-permute-start.1
  188.0 1.4 collective-permute-start.2
  188.0 3.6 collective-permute-start.3
  335.1 198.1 %copy-start.2 = (f32[6,128,128]{2,1,0:T(8,128)S(1)}, f32[6,128,128]{2,1,0:T(8,128)}, u32[]{:S(2)}) copy-start(f32[6,128,128]{2,1,0:T(8,128)} %get-tuple-element.173) | copy-start | bytes 1179652
  341.5 7.2 collective-permute-start.4
  343.1 5.5 collective-permute-start.5
  344.1 5.0 collective-permute-start.6
  348.3 3.2 collective-permute-start.7
  351.5 185.9 %copy-start = (f32[256,128]{1,0:T(8,128)S(1)}, f32[256,128]{1,0:T(8,128)}, u32[]{:S(2)}) copy-start(f32[256,128]{1,0:T(8,128)} %get-tuple-element.425) | copy-start | bytes 393220
  355.2 236.6 %all-gather.5.cloned.1.call-start = ((), (), s32[]{:S(2)}) async-start(), calls=%async_computation.1 | async-start | bytes 4227072 | tf_op jit(solution)/shard_map/all_gather | solution.py:213
  525.7 174.7 %all-gather.7.cloned.1.call-start = ((), (), s32[]{:S(2)}) async-start(), calls=%async_computation.2 | async-start | bytes 8454144 | tf_op jit(solution)/shard_map/all_gather | solution.py:37
Sparse Core Ops, SparseCore 0:
  182.9 152.1 all-reduce.9
  355.3 144.4 all-reduce.7
  525.8 65.9 all-gather.4
  632.7 67.5 all-gather.6
where the time goes:
time: 738 us; the launch traced here: 736 us
  waiting for transfers between devices  414 us (56%)
  matrix products  113 us (15%)
  blocking collectives  103 us (14%)
  other arithmetic  55 us (7%)
  between operations  14.3 us (2%)
  starting transfers between devices  12.9 us (2%)
  local copies, waits for them, and re-layouts  11.6 us (2%)
  loops' own time  11.5 us (2%)
    psum x1, waiting for transfers between devices, local(): reduced_all = lax.psum(local_sums * weight_x, ('slab', 'brick'))  145 us
    psum x1, waiting for transfers between devices, local(): transport, vectors = lax.psum((transport, vectors), ('slab', 'brick'))  143 us
    psum x1, blocking collectives, local(): transport, vectors = lax.psum((transport, vectors), ('slab', 'brick'))  68.7 us
    all_gather x1, waiting for transfers between devices, over_pieces(): parts = lax.all_gather(array, axis)  67.7 us
    all_gather x1, waiting for transfers between devices, local(): lax.all_gather(basis_new, ('slab', 'brick'), axis=0, tiled=True)  52.7 us
    dot_general x16, matrix products, one_block(): jnp.dot(maxwell(part_params, velocity), v_basis, precision=PRECISE)  38.9 us
    dot_general x16, matrix products, add_block(): lax.dot_general(values, basis_block, (((0,), (0,)), ((), ())), precision=...  37.2 us
    all_gather x1, blocking collectives, local(): lax.all_gather(cell_params, ('slab', 'brick'), axis=1, tiled=True)  34.4 us
  transfers between devices with their start and end apart: 12, of which 9 were waited for; matrix products, arithmetic and copies ran while one was open for 2% of the time, Pallas kernels for 0%

commit v1 on v0

--- a/solution.py
+++ b/solution.py
@@ -166,7 +166,8 @@
             for axis_id in range(3)
         ]
     )
-    transport, vectors = lax.psum((transport, vectors), ("slab", "brick"))
+    map_begin = lambda local_values: jax.lax.psum(jax.lax.psum(local_values, "slab"), "brick")
+    transport, vectors = map_begin((transport, vectors))
     coeff_flat = k_coeffs.reshape(cell_count, rank_size)
     cell_params = cell_state(vectors, coeff_flat)
     params_all = lax.all_gather(cell_params, ("slab", "brick"), axis=1, tiled=True)

time: 738 us -> 788 us (1.068)
  waiting for transfers between devices: 414 us -> 491 us
  blocking collectives: 103 us -> 85.6 us
  matrix products: 113 us -> 98.5 us
    psum x1 -> x3, waiting for transfers between devices: 143 us -> 223 us  [the longest x1 155 us: local(): lax.psum(blocks.reshape(row_total, rank_size), ('slab', 'brick'))]
    psum x1 -> x2, blocking collectives: 68.7 us -> 51.3 us  [the longest x1 32.3 us: local(): jax.lax.psum(jax.lax.psum(local_values, 'slab'), 'brick')]
    dot_general x16, matrix products: 38.9 us -> 24.4 us  [one_block(): jnp.dot(maxwell(part_params, velocity), v_basis, precision=PRECISE)]
  transfers between devices with their start and end apart: 12 -> 14, of which waited for: 9 -> 7; matrix products, arithmetic and copies ran while one was open for 2% -> 7% of each run, Pallas kernels for 0% -> 0%
where the time goes in v1:
time: 788 us; the launch traced here: 786 us
  waiting for transfers between devices  491 us (62%)
  matrix products  98.5 us (12%)
  blocking collectives  85.6 us (11%)
  other arithmetic  55 us (7%)
  starting transfers between devices  15.9 us (2%)
  between operations  14.7 us (2%)
  local copies, waits for them, and re-layouts  13.8 us (2%)
  loops' own time  11.5 us (1%)
    psum x1, waiting for transfers between devices, local(): lax.psum(blocks.reshape(row_total, rank_size), ('slab', 'brick'))  155 us
    psum x1, waiting for transfers between devices, local(): reduced_all = lax.psum(local_sums * weight_x, ('slab', 'brick'))  144 us
    psum x1, waiting for transfers between devices, local(): jax.lax.psum(jax.lax.psum(local_values, 'slab'), 'brick')  68.2 us
    all_gather x1, waiting for transfers between devices, over_pieces(): parts = lax.all_gather(array, axis)  67.7 us
    all_gather x1, waiting for transfers between devices, local(): lax.all_gather(basis_new, ('slab', 'brick'), axis=0, tiled=True)  52.7 us
    dot_general x16, matrix products, add_block(): lax.dot_general(values, basis_block, (((0,), (0,)), ((), ())), precision=...  37.2 us
    all_gather x1, blocking collectives, local(): lax.all_gather(cell_params, ('slab', 'brick'), axis=1, tiled=True)  34.3 us
    psum x1, blocking collectives, local(): jax.lax.psum(jax.lax.psum(local_values, 'slab'), 'brick')  32.3 us
  transfers between devices with their start and end apart: 14, of which 7 were waited for; matrix products, arithmetic and copies ran while one was open for 7% of the time, Pallas kernels for 0%

profile of v1, /device:TPU:1, one launch (start us, length us, event | category | flops | bytes accessed | tf_op | source)
XLA Modules:
  0.0 785.8 jit_solution(14760448923321212404)
XLA Ops:
  17.6 3.6 collective-permute-start
  21.2 2.5 collective-permute-start.1
  24.4 2.6 collective-permute-start.2
  28.1 19.0 %psum.44 = f32[5,128]{1,0:T(8,128)S(1)} all-reduce(f32[5,128]{1,0:T(8,128)S(1)} %convolution_multiply_fusion.9), channel_id=1, replica_groups=mesh['slab'=8,'brick'=16] {'slab'}, use_global_device_ids=true, to_apply=%region_3.4 | all-reduce | flops 640 | bytes 5120 | tf_op jit(solution)/shard_map/psum | solution.py:169
  47.1 32.3 %psum.45 = f32[5,128]{1,0:T(8,128)S(1)} all-reduce(f32[5,128]{1,0:T(8,128)S(1)} %psum.44), channel_id=1, replica_groups=mesh['slab'=8,'brick'=16] {'brick'}, use_global_device_ids=true, to_apply=%region_4.5 | all-reduce | flops 640 | bytes 5120 | tf_op jit(solution)/shard_map/psum | solution.py:169
  80.4 34.3 %all-gather.1 = f32[128,64,5]{1,2,0:T(8,128)S(1)} all-gather(f32[1,64,5]{1,2,0:T(8,128)S(1)} %maximum_bitcast_fusion), channel_id=1, replica_groups=mesh['slab'=8,'brick'=16] {'slab','brick'}, dimensions={0}, use_global_device_ids=true | all-gather | bytes 165120 | tf_op jit(solution)/shard_map/all_gather | solution.py:173
  115.0 46.0 %while.24 = (s32[]{:T(128)}, f32[16,512,128]{2,1,0:T(8,128)}, s32[16]{0:T(128)S(1)}, f32[5,8192]{1,0:T(8,128)S(1)}, f32[3,256]{1,0:T(4,128)S(1)}, /*index=5*/f32...) while((s32[]{:T(128)}, f32[16,512,128]{2,1,0:T(8,128)}, ...), condition=%wide.region_7.8_spmd, body=%wide.region_6.7_spmd.sunk | while | flops 202704400 | bytes 433923 | solution.py:183
  162.0 68.2 %all-reduce.11.cloned.1.call-done = f32[6,128,128]{2,1,0:T(8,128)} async-done(((f32[6,128,128]{2,1,0:T(8,128)}), f32[6,128,128]{2,1,0:T(8,128)}) %all-reduce.11.cloned.1.call-update) | async-done | bytes 393232 | tf_op jit(solution)/shard_map/psum | solution.py:169
  235.4 154.9 %all-reduce.13.cloned.1.call-done = f32[8192,128]{1,0:T(8,128)} async-done(((f32[8192,128]{1,0:T(8,128)}), f32[8192,128]{1,0:T(8,128)}) %all-reduce.13.cloned.1.call-update) | async-done | bytes 4194320 | tf_op jit(solution)/shard_map/psum | solution.py:184
  394.0 4.2 collective-permute-start.6
  405.3 144.4 %all-reduce.15.cloned.1.call-done = f32[8,128,128]{1,2,0:T(8,128)} async-done(((f32[8,128,128]{1,2,0:T(8,128)}), f32[8,128,128]{1,2,0:T(8,128)}) %all-reduce.15.cloned.1.call-update) | async-done | bytes 524304 | tf_op jit(solution)/shard_map/psum | solution.py:205
  551.5 11.7 %cholesky.44 = f32[128,128]{1,0:T(8,128)S(1)} custom-call(f32[128,128]{1,0:T(8,128)S(1)} %fusion.83), custom_call_target="Cholesky" | custom-call | tf_op jit(solution)/shard_map/jit(cholesky)/cholesky | solution.py:206
  564.5 9.8 %custom-call.7 = f32[1,128,128]{1,2,0:T(8,128)S(1)} custom-call(f32[1,128,128]{2,1,0:T(8,128)S(1)} %select_bitcast_fusion.1), custom_call_target="InvertDiagBlocksLowerTriangular" | custom-call | tf_op jit(solution)/shard_map/jit(_solve_triangular)/triangular_solve | solution.py:207
  589.0 52.7 %all-gather.5.cloned.1.call-done = f32[8192,128]{1,0:T(8,128)} async-done(((f32[64,128]{1,0:T(8,128)}), f32[8192,128]{1,0:T(8,128)}) %all-gather.5.cloned.1.call-update) | async-done | bytes 4194320 | tf_op jit(solution)/shard_map/all_gather | solution.py:214
  641.6 39.5 %while.25 = (s32[]{:T(128)}, f32[256,128]{1,0:T(8,128)S(1)}, f32[5,8192]{1,0:T(8,128)S(1)}, f32[3,256]{1,0:T(4,128)S(1)}, f32[8192,128]{1,0:T(8,128)}, /*index=5...) while((s32[]{:T(128)}, f32[256,128]{1,0:T(8,128)S(1)}, ...), condition=%wide.region_13.16_spmd.clone, body=%wide.region_12.15_spmd.clone.sunk | while | flops 202737168 | bytes 564477 | solution.py:229
  644.2 2.3 fusion.236
  646.7 2.3 fusion.236
  649.1 2.3 fusion.236
  651.6 2.3 fusion.236
  654.1 2.3 fusion.236
  682.4 67.7 %all-gather.7.cloned.1.call-done = f32[16384,128]{1,0:T(8,128)} async-done(((f32[128,128]{1,0:T(8,128)}), f32[16384,128]{1,0:T(8,128)}) %all-gather.7.cloned.1.call-update) | async-done | bytes 8388624 | tf_op jit(solution)/shard_map/all_gather | solution.py:37
  750.2 3.8 reduce_sum.32
  754.1 11.7 %cholesky.55 = f32[128,128]{1,0:T(8,128)S(1)} custom-call(f32[128,128]{1,0:T(8,128)S(1)} %fusion.85), custom_call_target="Cholesky" | custom-call | tf_op jit(solution)/shard_map/jit(cholesky)/cholesky | solution.py:241
  767.8 9.8 %custom-call.8 = f32[1,128,128]{1,2,0:T(8,128)S(1)} custom-call(f32[1,128,128]{2,1,0:T(8,128)S(1)} %get-tuple-element.173), custom_call_target="InvertDiagBlocksLowerTriangular" | custom-call | tf_op jit(solution)/shard_map/jit(_solve_triangular)/triangular_solve | solution.py:242
  (239 shorter events, 114.7 us)
Async XLA Ops:
  7.2 107.9 %copy-start = (f32[256,128]{1,0:T(8,128)S(1)}, f32[256,128]{1,0:T(8,128)}, u32[]{:S(2)}) copy-start(f32[256,128]{1,0:T(8,128)} %param.10) | copy-start | bytes 393220
  7.2 107.8 %all-reduce.9.cloned.1.call-start = ((), (), s32[]{:S(2)}) async-start(), calls=%async_computation | async-start | bytes 786432 | tf_op jit(solution)/shard_map/psum | solution.py:169
  16.0 0.8 copy-start.3
  16.8 213.4 %all-reduce.11.cloned.1.call-start = ((), (), s32[]{:S(2)}) async-start(), calls=%async_computation.1 | async-start | bytes 786432 | tf_op jit(solution)/shard_map/psum | solution.py:169
  17.6 144.2 %collective-permute-start = (f32[1,2,16,128]{3,2,1,0:T(8,128)S(1)}, f32[1,2,16,128]{3,2,1,0:T(8,128)S(1)}, u32[]{:S(2)}, u32[]{:S(2)}) collective-permute-start(f32[1,2,16,128]{3,2,1,0:T(8,128)S(1)} %get-tuple-element.220), channel_id=1, source_target_pairs={{0,16},{16,32},{32,48},{48,64},{64,80},{80,96},{96,112},{112,0},{1... | collective-permute-start | bytes 49160 | tf_op jit(solution)/shard_map/ppermute | solution.py:24
  21.2 140.7 %collective-permute-start.1 = (f32[1,2,16,128]{3,2,1,0:T(8,128)S(1)}, f32[1,2,16,128]{3,2,1,0:T(8,128)S(1)}, u32[]{:S(2)}, u32[]{:S(2)}) collective-permute-start(f32[1,2,16,128]{3,2,1,0:T(8,128)S(1)} %get-tuple-element.219), channel_id=1, source_target_pairs={{16,0},{32,16},{48,32},{64,48},{80,64},{96,80},{112,96},{0,112},{1... | collective-permute-start | bytes 49160 | tf_op jit(solution)/shard_map/ppermute | solution.py:25
  24.4 137.5 %collective-permute-start.2 = (f32[2,1,16,128]{3,2,1,0:T(8,128)S(1)}, f32[2,1,16,128]{3,2,1,0:T(8,128)S(1)}, u32[]{:S(2)}, u32[]{:S(2)}) collective-permute-start(f32[2,1,16,128]{3,2,1,0:T(8,128)S(1)} %get-tuple-element.218), channel_id=1, source_target_pairs={{0,1},{1,2},{2,3},{3,4},{4,5},{5,6},{6,7},{7,8},{8,9},{9,10},{10,1... | collective-permute-start | bytes 49160 | tf_op jit(solution)/shard_map/ppermute | solution.py:24
  27.0 134.9 %collective-permute-start.3 = (f32[2,1,16,128]{3,2,1,0:T(8,128)S(1)}, f32[2,1,16,128]{3,2,1,0:T(8,128)S(1)}, u32[]{:S(2)}, u32[]{:S(2)}) collective-permute-start(f32[2,1,16,128]{3,2,1,0:T(8,128)S(1)} %get-tuple-element.217), channel_id=1, source_target_pairs={{1,0},{2,1},{3,2},{4,3},{5,4},{6,5},{7,6},{8,7},{9,8},{10,9},{11,1... | collective-permute-start | bytes 49160 | tf_op jit(solution)/shard_map/ppermute | solution.py:25
  115.0 275.3 %all-reduce.13.cloned.1.call-start = ((), (), s32[]{:S(2)}) async-start(), calls=%async_computation.2 | async-start | bytes 8388608 | tf_op jit(solution)/shard_map/psum | solution.py:184
  161.1 0.8 copy-start.1
  161.1 388.6 %all-reduce.15.cloned.1.call-start = ((), (), s32[]{:S(2)}) async-start(), calls=%async_computation.3 | async-start | bytes 1048576 | tf_op jit(solution)/shard_map/psum | solution.py:205
  230.2 352.9 %copy-start.2 = (f32[6,128,128]{2,1,0:T(8,128)S(1)}, f32[6,128,128]{2,1,0:T(8,128)}, u32[]{:S(2)}) copy-start(f32[6,128,128]{2,1,0:T(8,128)} %all-reduce.11.cloned.1.call-done) | copy-start | bytes 1179652
  391.4 7.1 collective-permute-start.4
  393.0 5.5 collective-permute-start.5
  394.0 5.1 collective-permute-start.6
  398.2 3.2 collective-permute-start.7
  405.1 236.6 %all-gather.5.cloned.1.call-start = ((), (), s32[]{:S(2)}) async-start(), calls=%async_computation.4 | async-start | bytes 4227072 | tf_op jit(solution)/shard_map/all_gather | solution.py:214
  575.5 174.7 %all-gather.7.cloned.1.call-start = ((), (), s32[]{:S(2)}) async-start(), calls=%async_computation.5 | async-start | bytes 8454144 | tf_op jit(solution)/shard_map/all_gather | solution.py:37
Sparse Core Ops, SparseCore 0:
  16.9 83.0 all-reduce.8
  115.1 115.0 all-reduce.10
  235.1 155.1 all-reduce.12
  405.2 144.4 all-reduce.14
  575.6 65.9 all-gather.4
  682.6 67.5 all-gather.6
